TPU v7x, 256 devices: a whole 4x4x8 slice. The times are simulated.
256 devices in a mesh: grp: 2 (over z_lo), gx: 64 (over x, z_hi, y), gz: 2 (over core).
Axes of the slice: x: 4, y: 4, z: 8 (z_hi: 4, z_lo: 2; z = z_hi * 2 + z_lo), core: 2. Of those that a mesh axis runs over, the one named last changes fastest.
Arguments:
- fields: float32 [4, 2, 4, 4096, 1024], P(None, 'grp', None, 'gx', 'gz'), may hold values from -4 to 4
- buoyancy: float32 [2, 4, 4096, 1024], P('grp', None, 'gx', 'gz'), may hold values from 0.3 to 0.9
- stiffness: float32 [2, 4, 4096, 1024], P('grp', None, 'gx', 'gz'), may hold values from 0.2 to 0.7
- stress_zero: float32 [4096, 1024], P('gx', 'gz'), may hold values from -5 to 5
- direct_effect: float32 [4096, 1024], P('gx', 'gz'), may hold values from 1 to 8
- log_state: float32 [4096, 1024], P('gx', 'gz'), may hold values from -2 to 2
- kernel: float32 [16, 1024, 4096], P(None, ('grp', 'gx', 'gz')), may hold values from -2 to 2
- history: float32 [16, 1024, 2, 4096], P(None, ('grp', 'gx', 'gz')), may hold values from -5 to 5
- truncation: int32 [1024, 4096], P(('grp', 'gx', 'gz')), may hold values from 1 to 16
Outputs:
- fields_next: float32 [4, 2, 4, 4096, 1024], P(None, 'grp', None, 'gx', 'gz')
- state_next: float32 [4096, 1024], P('gx', 'gz')
- spectra_new: float32 [4, 1024, 2, 4096], P(None, ('grp', 'gx', 'gz'))
All inputs are finite; a program needn't handle non-finite values.
Results may differ from a plain program's by a relative error of at most 0.0003.
Values sent between devices are 32-bit elements; how exact they have to be, the bound alone decides.
A program may use at most 128 MiB of HBM per device.

v0:
```python
import math
import jax
import jax.numpy as jnp
from jax import lax
from jax.sharding import PartitionSpec as P

NSTEP = 4
NEWTON = 4
FACE_NEAR = 9.0 / 8.0
FACE_FAR = 1.0 / 24.0
DAMPING = 1.0
FULL_PRECISION = lax.Precision.HIGHEST


def extended(cells, sides, width):
    for axis, dim in sides:
        count = lax.axis_size(axis)
        ends = count - 1
        head = lax.slice_in_dim(cells, 0, width, axis=dim)
        tail = lax.slice_in_dim(cells, cells.shape[dim] - width, cells.shape[dim], axis=dim)
        cells = jnp.concatenate(
            [
                lax.ppermute(tail, axis, [(i, (i + 1) % count) for i in range(ends)]),
                cells,
                lax.ppermute(head, axis, [((i + 1) % count, i) for i in range(ends)]),
            ],
            axis=dim,
        )
    return cells


def from_partner(x, axis, stride):
    return lax.ppermute(x, axis, [(i, i ^ 1 << stride) for i in range(lax.axis_size(axis))])


def stencil(values, axis_index, pad_before, pad_after):
    widths = [(0, 0)] * values.ndim
    widths[axis_index] = (pad_before, pad_after)
    padded = jnp.pad(values, widths)
    length = values.shape[axis_index]

    def window(offset):
        return lax.slice_in_dim(padded, offset, offset + length, axis=axis_index)

    return FACE_NEAR * (window(2) - window(1)) - FACE_FAR * (window(3) - window(0))


def margin_stencil(padded, axis_index, length, lead_cells):

    def window(offset):
        return lax.slice_in_dim(
            padded, lead_cells + offset, lead_cells + offset + length, axis=axis_index
        )

    return FACE_NEAR * (window(2) - window(1)) - FACE_FAR * (window(3) - window(0))


def inverse_sinh(scaled):
    magnitude = jnp.abs(scaled)
    positive = jnp.log(magnitude + jnp.sqrt(1.0 + magnitude * magnitude))
    return jnp.where(scaled < 0.0, -positive, positive)


def friction(loading, direct_effect, log_state, initial):
    factor = jnp.exp(log_state)
    slip_rate = initial
    for repeat in range(NEWTON):
        scaled = slip_rate * factor
        misfit = direct_effect * inverse_sinh(scaled) + DAMPING * slip_rate - loading
        slope_total = direct_effect * factor / jnp.sqrt(1.0 + scaled * scaled) + DAMPING
        slip_rate = slip_rate - misfit / slope_total
    return slip_rate


def phase_table(first_index, second_index, length, direction):
    turn_count = first_index * second_index % length
    angle_value = turn_count.astype(jnp.float32) * (2.0 * math.pi / length)
    return (jnp.cos(angle_value), direction * jnp.sin(angle_value))


def complex_apply(real_part, imag_part, cos_table, sin_table, formula):
    real_cos = jnp.einsum(formula, real_part, cos_table, precision=FULL_PRECISION)
    imag_sin = jnp.einsum(formula, imag_part, sin_table, precision=FULL_PRECISION)
    real_sin = jnp.einsum(formula, real_part, sin_table, precision=FULL_PRECISION)
    imag_cos = jnp.einsum(formula, imag_part, cos_table, precision=FULL_PRECISION)
    return (real_cos - imag_sin, real_sin + imag_cos)


def strike_forward(values, outer_count, inner_count):
    planes_count = values.shape[0]
    total_count = outer_count * inner_count
    real_part = values[:, 0].reshape(planes_count, outer_count, inner_count)
    imag_part = values[:, 1].reshape(planes_count, outer_count, inner_count)
    outer_iota = jnp.arange(outer_count, dtype=jnp.int32)
    inner_iota = jnp.arange(inner_count, dtype=jnp.int32)
    cos_table, sin_table = phase_table(outer_iota[:, None], outer_iota[None, :], outer_count, -1.0)
    real_part, imag_part = complex_apply(real_part, imag_part, cos_table, sin_table, "rab,ak->rkb")
    cos_table, sin_table = phase_table(outer_iota[:, None], inner_iota[None, :], total_count, -1.0)
    real_part, imag_part = (
        real_part * cos_table - imag_part * sin_table,
        real_part * sin_table + imag_part * cos_table,
    )
    cos_table, sin_table = phase_table(inner_iota[:, None], inner_iota[None, :], inner_count, -1.0)
    real_part, imag_part = complex_apply(real_part, imag_part, cos_table, sin_table, "rkb,bm->rmk")
    return jnp.stack(
        [
            real_part.reshape(planes_count, total_count),
            imag_part.reshape(planes_count, total_count),
        ],
        axis=1,
    )


def strike_inverse(values, outer_count, inner_count):
    planes_count = values.shape[0]
    total_count = outer_count * inner_count
    real_part = values[:, 0].reshape(planes_count, inner_count, outer_count)
    imag_part = values[:, 1].reshape(planes_count, inner_count, outer_count)
    outer_iota = jnp.arange(outer_count, dtype=jnp.int32)
    inner_iota = jnp.arange(inner_count, dtype=jnp.int32)
    cos_table, sin_table = phase_table(inner_iota[:, None], inner_iota[None, :], inner_count, 1.0)
    real_part, imag_part = complex_apply(real_part, imag_part, cos_table, sin_table, "rmk,mb->rkb")
    cos_table, sin_table = phase_table(outer_iota[:, None], inner_iota[None, :], total_count, 1.0)
    real_part, imag_part = (
        real_part * cos_table - imag_part * sin_table,
        real_part * sin_table + imag_part * cos_table,
    )
    cos_table, sin_table = phase_table(outer_iota[:, None], outer_iota[None, :], outer_count, 1.0)
    real_part, imag_part = complex_apply(real_part, imag_part, cos_table, sin_table, "rkb,ka->rab")
    return jnp.stack(
        [
            real_part.reshape(planes_count, total_count),
            imag_part.reshape(planes_count, total_count),
        ],
        axis=1,
    )


def per_device(
    fields, buoyancy, stiffness, stress_zero, direct_effect, log_state, kernel, history, truncation
):
    side_index = lax.axis_index("grp")
    on_plus = side_index == 1
    depth_index = lax.axis_index("gz")
    strike_devices = lax.axis_size("gx")
    depth_devices = lax.axis_size("gz")
    velocity = fields[0]
    normal_stress = fields[1]
    shear_stress = fields[2:4]
    strike_rows = velocity.shape[2]
    depth_cols = velocity.shape[3]
    modes_dev = history.shape[1]
    strike_total = history.shape[3]
    depth_total = depth_cols * depth_devices
    mode_rows = strike_devices * modes_dev
    scale_back = 1.0 / math.sqrt(strike_total * depth_total)
    lag_number = lax.broadcasted_iota(jnp.int32, kernel.shape, 0)
    weights = jnp.where(lag_number < truncation[None], kernel, jnp.zeros_like(kernel))

    def mode_numbers(row_index, depth_part):
        return (
            (side_index * strike_devices + row_index // modes_dev) * depth_devices + depth_part
        ) * modes_dev + row_index % modes_dev

    own_modes = mode_numbers(jnp.arange(mode_rows, dtype=jnp.int32), depth_index)
    depth_iota = jnp.arange(depth_total, dtype=jnp.int32)
    back_cos, back_sin = phase_table(own_modes[:, None], depth_iota[None, :], depth_total, 1.0)
    lagged = history
    spectra = []
    for step_number in range(NSTEP):
        summed = jnp.sum(weights[:, :, None, :] * lagged, axis=0)
        in_space = strike_inverse(summed, strike_devices, strike_rows)
        by_rows = lax.all_to_all(in_space, "gx", split_axis=2, concat_axis=0, tiled=True)
        partial_value = jnp.einsum(
            "jy,jz->yz", by_rows[:, 0], back_cos, precision=FULL_PRECISION
        ) - jnp.einsum("jy,jz->yz", by_rows[:, 1], back_sin, precision=FULL_PRECISION)
        own_depth = lax.psum_scatter(partial_value, "gz", scatter_dimension=1, tiled=True)
        relief = lax.psum(own_depth, "grp") * scale_back
        padded = extended(velocity, (("gx", 2), ("gz", 3)), 2)
        normal_stress = normal_stress + stiffness * stencil(velocity, 1, 2, 1)
        strike_grad = margin_stencil(padded[:, :, :, 2 : 2 + depth_cols], 2, strike_rows, 1)
        depth_grad = margin_stencil(padded[:, :, 2 : 2 + strike_rows, :], 3, depth_cols, 1)
        shear_stress = shear_stress + stiffness * jnp.stack([strike_grad, depth_grad])
        near_plane = velocity[0, 0]
        far_plane = from_partner(near_plane, "grp", 0)
        velocity_plus = jnp.where(on_plus, near_plane, far_plane)
        velocity_minus = jnp.where(on_plus, far_plane, near_plane)
        slip_guess = velocity_plus - velocity_minus
        loading = stress_zero + relief + DAMPING * slip_guess
        slip_rate = friction(loading, direct_effect, log_state, slip_guess)
        traction = loading - DAMPING * slip_rate
        log_state = 0.75 * log_state - 0.2 * jnp.log(1.0 + slip_rate * slip_rate) + 0.1
        normal_stress = normal_stress.at[0, 0].set(jnp.where(on_plus, traction, -traction))
        shear_rim = extended(shear_stress, (("gx", 3), ("gz", 4)), 2)
        strike_div = margin_stencil(shear_rim[0][:, :, :, 2 : 2 + depth_cols], 2, strike_rows, 0)
        depth_div = margin_stencil(shear_rim[1][:, :, 2 : 2 + strike_rows, :], 3, depth_cols, 0)
        velocity = velocity + buoyancy * (stencil(normal_stress, 1, 1, 2) + strike_div + depth_div)
        term_index = jnp.arange(mode_rows * lax.axis_size("gz"), dtype=jnp.int32)
        term_modes = mode_numbers(term_index % mode_rows, term_index // mode_rows)
        depth_here = depth_index * depth_cols + jnp.arange(depth_cols, dtype=jnp.int32)
        cos_part, sin_part = phase_table(
            term_modes[:, None], depth_here[None, :], depth_total, -1.0
        )
        real_term = jnp.einsum("jz,yz->jy", cos_part, slip_rate, precision=FULL_PRECISION)
        imag_term = jnp.einsum("jz,yz->jy", sin_part, slip_rate, precision=FULL_PRECISION)
        by_modes = lax.psum_scatter(
            jnp.stack([real_term, imag_term], axis=1), "gz", scatter_dimension=0, tiled=True
        )
        spread = lax.all_to_all(by_modes, "gx", split_axis=0, concat_axis=2, tiled=True)
        fresh_modes = strike_forward(spread, strike_devices, strike_rows) * scale_back
        spectra.append(fresh_modes)
        lagged = jnp.concatenate([fresh_modes[None], lagged[:-1]], axis=0)
    return (
        jnp.stack([velocity, normal_stress, shear_stress[0], shear_stress[1]]),
        log_state,
        jnp.stack(spectra),
    )


def solution(mesh):
    return jax.shard_map(
        per_device,
        mesh=mesh,
        in_specs=(
            P(None, "grp", None, "gx", "gz"),
            P("grp", None, "gx", "gz"),
            P("grp", None, "gx", "gz"),
            P("gx", "gz"),
            P("gx", "gz"),
            P("gx", "gz"),
            P(None, ("grp", "gx", "gz"), None),
            P(None, ("grp", "gx", "gz"), None, None),
            P(("grp", "gx", "gz"), None),
        ),
        out_specs=(
            P(None, "grp", None, "gx", "gz"),
            P("gx", "gz"),
            P(None, ("grp", "gx", "gz"), None, None),
        ),
        check_vma=False,
    )
```

profile of v0, /device:TPU:1, one launch (start us, length us, event | category | flops | bytes accessed | tf_op | source)
XLA Modules:
  0.0 803.6 jit_solution(6997939394833421156)
XLA Ops:
  26.4 7.4 reshape.589
  33.9 18.6 %all-to-all-start = ((f32[64,1,512]{2,1,0:T(1,128)}), f32[64,1,512]{2,1,0:T(1,128)S(1)}, u32[]{:S(2)}, u32[]{:S(2)}) async-start(f32[64,1,512]{2,1,0:T(1,128)} %reshape.589), calls=%async_computation | async-start | bytes 262144 | tf_op jit(solution)/shard_map/all_to_all | solution.py:173
  69.9 7.9 reshape.590
  77.8 5.4 copy.332
  88.0 5.4 convolution_subtract_fusion.3
  94.1 10.1 %collective-permute-start = (f32[64,512]{1,0:T(8,128)}, f32[64,512]{1,0:T(8,128)}, u32[]{:S(2)}, u32[]{:S(2)}) collective-permute-start(f32[64,512]{1,0:T(8,128)} %slice_bitcast_fusion.24), channel_id=1, source_target_pairs={{0,128},{128,0},{1,129},{129,1},{2,130},{130,2},{3,131},{131,3},{4... | collective-permute-start | bytes 393224 | tf_op jit(solution)/shard_map/ppermute | solution.py:33
  117.8 33.4 %all-reduce.13.cloned.1.call-done = f32[64,512]{1,0:T(8,128)} async-done(((f32[64,512]{1,0:T(8,128)}), f32[64,512]{1,0:T(8,128)}) %all-reduce.13.cloned.1.call-update) | async-done | bytes 131088 | tf_op jit(solution)/shard_map/psum | solution.py:178
  153.4 5.0 convolution_bitcast_fusion.6
  158.4 4.9 convolution_bitcast_fusion.7
  175.6 5.2 collective-permute-start.12
  187.7 17.2 %all-to-all-start.1 = ((f32[64,1,512]{2,1,0:T(1,128)}), f32[64,1,512]{2,1,0:T(1,128)S(1)}, u32[]{:S(2)}, u32[]{:S(2)}) async-start(f32[64,1,512]{2,1,0:T(1,128)} %reshape.591), calls=%async_computation.3 | async-start | bytes 262144 | tf_op jit(solution)/shard_map/all_to_all | solution.py:209
  208.3 8.1 %all-to-all-done.1 = f32[64,1,512]{2,1,0:T(1,128)S(1)} async-done(((f32[64,1,512]{2,1,0:T(1,128)}), f32[64,1,512]{2,1,0:T(1,128)S(1)}, u32[]{:S(2)}, u32[]{:S(2)}) %all-to-all-start.1) | async-done | bytes 131104 | tf_op jit(solution)/shard_map/all_to_all | solution.py:209
  260.6 7.4 reshape.593
  285.0 8.0 reshape.594
  293.0 5.4 copy.337
  303.1 5.4 convolution_subtract_fusion.2
  311.2 6.3 collective-permute-start.17
  328.1 32.7 %all-reduce.15.cloned.1.call-done = f32[64,512]{1,0:T(8,128)} async-done(((f32[64,512]{1,0:T(8,128)}), f32[64,512]{1,0:T(8,128)}) %all-reduce.15.cloned.1.call-update) | async-done | bytes 131088 | tf_op jit(solution)/shard_map/psum | solution.py:178
  362.9 5.0 convolution_bitcast_fusion.4
  367.9 4.9 convolution_bitcast_fusion.5
  391.2 7.4 reduce-scatter.15.cloned.1.call-done
  402.2 12.6 %all-to-all-start.3 = ((f32[64,1,512]{2,1,0:T(1,128)}), f32[64,1,512]{2,1,0:T(1,128)}, u32[]{:S(2)}, u32[]{:S(2)}) async-start(f32[64,1,512]{2,1,0:T(1,128)} %reshape.595), calls=%async_computation.7 | async-start | bytes 262144 | tf_op jit(solution)/shard_map/all_to_all | solution.py:209
  418.1 8.6 %all-to-all-done.3 = f32[64,1,512]{2,1,0:T(1,128)} async-done(((f32[64,1,512]{2,1,0:T(1,128)}), f32[64,1,512]{2,1,0:T(1,128)}, u32[]{:S(2)}, u32[]{:S(2)}) %all-to-all-start.3) | async-done | bytes 131104 | tf_op jit(solution)/shard_map/all_to_all | solution.py:209
  454.8 7.5 reshape.597
  462.3 5.5 all-to-all-start.4
  480.8 8.3 %reshape.598 = f32[4096,2,4]{2,1,0:T(2,128)} reshape(f32[64,512]{1,0:T(8,128)S(1)} %reduce.44) | data formatting | bytes 262144
  489.1 5.4 copy.342
  499.3 5.4 convolution_subtract_fusion.1
  516.1 4.9 reduce-scatter.17.cloned.1.call-done
  523.7 32.8 %all-reduce.17.cloned.1.call-done = f32[64,512]{1,0:T(8,128)} async-done(((f32[64,512]{1,0:T(8,128)}), f32[64,512]{1,0:T(8,128)}) %all-reduce.17.cloned.1.call-update) | async-done | bytes 131088 | tf_op jit(solution)/shard_map/psum | solution.py:178
  558.7 5.0 convolution_bitcast_fusion.2
  563.7 4.9 convolution_bitcast_fusion.3
  581.2 5.3 collective-permute-start.30
  588.4 17.2 %all-to-all-start.5 = ((f32[64,1,512]{2,1,0:T(1,128)}), f32[64,1,512]{2,1,0:T(1,128)S(1)}, u32[]{:S(2)}, u32[]{:S(2)}) async-start(f32[64,1,512]{2,1,0:T(1,128)} %reshape.599), calls=%async_computation.11 | async-start | bytes 262144 | tf_op jit(solution)/shard_map/all_to_all | solution.py:209
  612.3 5.3 all-to-all-done.5
  639.7 7.5 reshape.601
  647.2 6.9 all-to-all-start.6
  656.8 8.7 %all-to-all-done.6 = f32[64,1,512]{2,1,0:T(1,128)S(1)} async-done(((f32[64,1,512]{2,1,0:T(1,128)}), f32[64,1,512]{2,1,0:T(1,128)S(1)}, u32[]{:S(2)}, u32[]{:S(2)}) %all-to-all-start.6) | async-done | bytes 131104 | tf_op jit(solution)/shard_map/all_to_all | solution.py:173
  666.5 7.9 reshape.602
  674.4 5.4 copy.347
  684.6 5.4 convolution_subtract_fusion
  702.5 6.5 collective-permute-start.35
  709.1 25.8 %all-reduce.19.cloned.1.call-done = f32[64,512]{1,0:T(8,128)} async-done(((f32[64,512]{1,0:T(8,128)}), f32[64,512]{1,0:T(8,128)}) %all-reduce.19.cloned.1.call-update) | async-done | bytes 131088 | tf_op jit(solution)/shard_map/psum | solution.py:178
  737.1 5.0 convolution_bitcast_fusion
  742.1 4.9 convolution_bitcast_fusion.1
  750.1 12.4 %reduce-scatter.23.cloned.1.call-done = f32[256,2,64]{0,2,1:T(8,128)} async-done(((f32[512,2,64]{0,2,1:T(8,128)}), f32[256,2,64]{0,2,1:T(8,128)}) %reduce-scatter.23.cloned.1.call-update) | async-done | bytes 131088 | tf_op jit(solution)/shard_map/reduce_scatter | solution.py:206
  764.5 12.3 %all-to-all-start.7 = ((f32[64,1,512]{2,1,0:T(1,128)}), f32[64,1,512]{2,1,0:T(1,128)S(1)}, u32[]{:S(2)}, u32[]{:S(2)}) async-start(f32[64,1,512]{2,1,0:T(1,128)} %reshape.603), calls=%async_computation.15 | async-start | bytes 262144 | tf_op jit(solution)/shard_map/all_to_all | solution.py:209
  783.2 5.7 all-to-all-done.7
  (429 shorter events, 333.5 us)
Async XLA Ops:
  8.4 44.1 %collective-permute-start.1 = (f32[1,4,2,512]{3,2,1,0:T(2,128)S(1)}, f32[1,4,2,512]{3,2,1,0:T(2,128)S(1)}, u32[]{:S(2)}, u32[]{:S(2)}) collective-permute-start(f32[1,4,2,512]{3,2,1,0:T(2,128)S(1)} %get-tuple-element.127), channel_id=1, source_target_pairs={{2,0},{4,2},{6,4},{8,6},{10,8},{12,10},{14,12},{16,14},{18,16},{20... | collective-permute-start | bytes 49160 | tf_op jit(solution)/shard_map/ppermute | solution.py:25
  9.7 42.8 %collective-permute-start.2 = (f32[1,4,2,512]{3,2,1,0:T(2,128)S(1)}, f32[1,4,2,512]{3,2,1,0:T(2,128)S(1)}, u32[]{:S(2)}, u32[]{:S(2)}) collective-permute-start(f32[1,4,2,512]{3,2,1,0:T(2,128)S(1)} %get-tuple-element.126), channel_id=1, source_target_pairs={{0,2},{2,4},{4,6},{6,8},{8,10},{10,12},{12,14},{14,16},{16,18},{18... | collective-permute-start | bytes 49160 | tf_op jit(solution)/shard_map/ppermute | solution.py:23
  33.9 34.6 %all-to-all-start = ((f32[64,1,512]{2,1,0:T(1,128)}), f32[64,1,512]{2,1,0:T(1,128)S(1)}, u32[]{:S(2)}, u32[]{:S(2)}) async-start(f32[64,1,512]{2,1,0:T(1,128)} %reshape.589), calls=%async_computation | async-start | bytes 262144 | tf_op jit(solution)/shard_map/all_to_all | solution.py:173
  52.5 62.6 %reduce-scatter.9.cloned.1.call-start = ((), (), s32[]{:S(2)}) async-start(), calls=%async_computation.16 | async-start | bytes 393216 | tf_op jit(solution)/shard_map/reduce_scatter | solution.py:177
  63.7 40.4 %collective-permute-start.5 = (f32[2,1,4,2,512]{4,3,2,1,0:T(2,128)}, f32[2,1,4,2,512]{4,3,2,1,0:T(2,128)S(1)}, u32[]{:S(2)}, u32[]{:S(2)}) collective-permute-start(f32[2,1,4,2,512]{4,3,2,1,0:T(2,128)} %get-tuple-element.98), channel_id=1, source_target_pairs={{0,2},{2,4},{4,6},{6,8},{8,10},{10,12},{12,14},{14,16},{16,18},{18... | collective-permute-start | bytes 98312 | tf_op jit(solution)/shard_map/ppermute | solution.py:23
  66.9 37.2 %collective-permute-start.6 = (f32[2,1,4,2,512]{4,3,2,1,0:T(2,128)}, f32[2,1,4,2,512]{4,3,2,1,0:T(2,128)S(1)}, u32[]{:S(2)}, u32[]{:S(2)}) collective-permute-start(f32[2,1,4,2,512]{4,3,2,1,0:T(2,128)} %get-tuple-element.99), channel_id=1, source_target_pairs={{2,0},{4,2},{6,4},{8,6},{10,8},{12,10},{14,12},{16,14},{18,16},{20... | collective-permute-start | bytes 98312 | tf_op jit(solution)/shard_map/ppermute | solution.py:25
  93.4 57.8 %all-reduce.13.cloned.1.call-start = ((), (), s32[]{:S(2)}) async-start(), calls=%async_computation.17 | async-start | bytes 262144 | tf_op jit(solution)/shard_map/psum | solution.py:178
  94.1 23.7 %collective-permute-start = (f32[64,512]{1,0:T(8,128)}, f32[64,512]{1,0:T(8,128)}, u32[]{:S(2)}, u32[]{:S(2)}) collective-permute-start(f32[64,512]{1,0:T(8,128)} %slice_bitcast_fusion.24), channel_id=1, source_target_pairs={{0,128},{128,0},{1,129},{129,1},{2,130},{130,2},{3,131},{131,3},{4... | collective-permute-start | bytes 393224 | tf_op jit(solution)/shard_map/ppermute | solution.py:33
  115.2 70.6 %reduce-scatter.11.cloned.1.call-start = ((), (), s32[]{:S(2)}) async-start(), calls=%async_computation.18 | async-start | bytes 393216 | tf_op jit(solution)/shard_map/reduce_scatter | solution.py:206
  168.7 5.3 collective-permute-start.10
  175.6 8.3 %collective-permute-start.12 = (f32[1,4,68,2]{3,2,1,0:T(8,128)S(1)}, f32[1,4,68,2]{3,2,1,0:T(8,128)}, u32[]{:S(2)}, u32[]{:S(2)}) collective-permute-start(f32[1,4,68,2]{3,2,1,0:T(8,128)S(1)} %get-tuple-element.110), channel_id=1, source_target_pairs={{1,0},{3,2},{5,4},{7,6},{9,8},{11,10},{13,12},{15,14},{17,16},{19,... | collective-permute-start | bytes 6536 | tf_op jit(solution)/shard_map/ppermute | solution.py:25
  182.6 22.4 %collective-permute-start.13 = (f32[1,4,68,2]{3,2,1,0:T(8,128)}, f32[1,4,68,2]{3,2,1,0:T(8,128)}, u32[]{:S(2)}, u32[]{:S(2)}) collective-permute-start(f32[1,4,68,2]{3,2,1,0:T(8,128)} %get-tuple-element.111), channel_id=1, source_target_pairs={{0,1},{2,3},{4,5},{6,7},{8,9},{10,11},{12,13},{14,15},{16,17},{18,... | collective-permute-start | bytes 6536 | tf_op jit(solution)/shard_map/ppermute | solution.py:23
  187.7 28.6 %all-to-all-start.1 = ((f32[64,1,512]{2,1,0:T(1,128)}), f32[64,1,512]{2,1,0:T(1,128)S(1)}, u32[]{:S(2)}, u32[]{:S(2)}) async-start(f32[64,1,512]{2,1,0:T(1,128)} %reshape.591), calls=%async_computation.3 | async-start | bytes 262144 | tf_op jit(solution)/shard_map/all_to_all | solution.py:209
  268.0 16.0 %all-to-all-start.2 = ((f32[64,1,512]{2,1,0:T(1,128)}), f32[64,1,512]{2,1,0:T(1,128)S(1)}, u32[]{:S(2)}, u32[]{:S(2)}) async-start(f32[64,1,512]{2,1,0:T(1,128)} %reshape.593), calls=%async_computation.4 | async-start | bytes 262144 | tf_op jit(solution)/shard_map/all_to_all | solution.py:173
  272.6 52.8 %reduce-scatter.13.cloned.1.call-start = ((), (), s32[]{:S(2)}) async-start(), calls=%async_computation.19 | async-start | bytes 393216 | tf_op jit(solution)/shard_map/reduce_scatter | solution.py:177
  275.7 32.9 %collective-permute-start.14 = (f32[2,1,4,2,512]{4,3,2,1,0:T(2,128)S(1)}, f32[2,1,4,2,512]{4,3,2,1,0:T(2,128)S(1)}, u32[]{:S(2)}, u32[]{:S(2)}) collective-permute-start(f32[2,1,4,2,512]{4,3,2,1,0:T(2,128)S(1)} %get-tuple-element.96), channel_id=1, source_target_pairs={{0,2},{2,4},{4,6},{6,8},{8,10},{10,12},{12,14},{14,16},{16,18},{18... | collective-permute-start | bytes 98312 | tf_op jit(solution)/shard_map/ppermute | solution.py:23
  278.5 30.1 %collective-permute-start.15 = (f32[2,1,4,2,512]{4,3,2,1,0:T(2,128)S(1)}, f32[2,1,4,2,512]{4,3,2,1,0:T(2,128)S(1)}, u32[]{:S(2)}, u32[]{:S(2)}) collective-permute-start(f32[2,1,4,2,512]{4,3,2,1,0:T(2,128)S(1)} %get-tuple-element.97), channel_id=1, source_target_pairs={{2,0},{4,2},{6,4},{8,6},{10,8},{12,10},{14,12},{16,14},{18,16},{20... | collective-permute-start | bytes 98312 | tf_op jit(solution)/shard_map/ppermute | solution.py:25
  308.5 52.2 %all-reduce.15.cloned.1.call-start = ((), (), s32[]{:S(2)}) async-start(), calls=%async_computation.20 | async-start | bytes 262144 | tf_op jit(solution)/shard_map/psum | solution.py:178
  309.9 8.8 %collective-permute-start.16 = (f32[2,1,4,68,2]{4,3,2,1,0:T(8,128)S(1)}, f32[2,1,4,68,2]{4,3,2,1,0:T(8,128)S(1)}, u32[]{:S(2)}, u32[]{:S(2)}) collective-permute-start(f32[2,1,4,68,2]{4,3,2,1,0:T(8,128)S(1)} %get-tuple-element.88), channel_id=1, source_target_pairs={{0,1},{2,3},{4,5},{6,7},{8,9},{10,11},{12,13},{14,15},{16,17},{18,... | collective-permute-start | bytes 13064 | tf_op jit(solution)/shard_map/ppermute | solution.py:23
  311.2 7.5 collective-permute-start.17
  317.5 10.5 %collective-permute-start.9 = (f32[64,512]{1,0:T(8,128)S(1)}, f32[64,512]{1,0:T(8,128)S(1)}, u32[]{:S(2)}, u32[]{:S(2)}) collective-permute-start(f32[64,512]{1,0:T(8,128)S(1)} %slice_bitcast_fusion.19), channel_id=1, source_target_pairs={{0,128},{128,0},{1,129},{129,1},{2,130},{130,2},{3,131},{131,3},{4... | collective-permute-start | bytes 393224 | tf_op jit(solution)/shard_map/ppermute | solution.py:33
  325.5 73.1 %reduce-scatter.15.cloned.1.call-start = ((), (), s32[]{:S(2)}) async-start(), calls=%async_computation.21 | async-start | bytes 393216 | tf_op jit(solution)/shard_map/reduce_scatter | solution.py:206
  373.9 6.1 collective-permute-start.19
  380.9 9.4 %collective-permute-start.21 = (f32[1,4,68,2]{3,2,1,0:T(8,128)S(1)}, f32[1,4,68,2]{3,2,1,0:T(8,128)S(1)}, u32[]{:S(2)}, u32[]{:S(2)}) collective-permute-start(f32[1,4,68,2]{3,2,1,0:T(8,128)S(1)} %get-tuple-element.106), channel_id=1, source_target_pairs={{1,0},{3,2},{5,4},{7,6},{9,8},{11,10},{13,12},{15,14},{17,16},{19,... | collective-permute-start | bytes 6536 | tf_op jit(solution)/shard_map/ppermute | solution.py:25
  388.8 26.0 %collective-permute-start.22 = (f32[1,4,68,2]{3,2,1,0:T(8,128)}, f32[1,4,68,2]{3,2,1,0:T(8,128)}, u32[]{:S(2)}, u32[]{:S(2)}) collective-permute-start(f32[1,4,68,2]{3,2,1,0:T(8,128)} %get-tuple-element.107), channel_id=1, source_target_pairs={{0,1},{2,3},{4,5},{6,7},{8,9},{10,11},{12,13},{14,15},{16,17},{18,... | collective-permute-start | bytes 6536 | tf_op jit(solution)/shard_map/ppermute | solution.py:23
  402.2 24.5 %all-to-all-start.3 = ((f32[64,1,512]{2,1,0:T(1,128)}), f32[64,1,512]{2,1,0:T(1,128)}, u32[]{:S(2)}, u32[]{:S(2)}) async-start(f32[64,1,512]{2,1,0:T(1,128)} %reshape.595), calls=%async_computation.7 | async-start | bytes 262144 | tf_op jit(solution)/shard_map/all_to_all | solution.py:209
  462.3 16.7 %all-to-all-start.4 = ((f32[64,1,512]{2,1,0:T(1,128)}), f32[64,1,512]{2,1,0:T(1,128)}, u32[]{:S(2)}, u32[]{:S(2)}) async-start(f32[64,1,512]{2,1,0:T(1,128)} %reshape.597), calls=%async_computation.8 | async-start | bytes 262144 | tf_op jit(solution)/shard_map/all_to_all | solution.py:173
  467.7 53.3 %reduce-scatter.17.cloned.1.call-start = ((), (), s32[]{:S(2)}) async-start(), calls=%async_computation.22 | async-start | bytes 393216 | tf_op jit(solution)/shard_map/reduce_scatter | solution.py:177
  471.8 32.9 %collective-permute-start.23 = (f32[2,1,4,2,512]{4,3,2,1,0:T(2,128)}, f32[2,1,4,2,512]{4,3,2,1,0:T(2,128)S(1)}, u32[]{:S(2)}, u32[]{:S(2)}) collective-permute-start(f32[2,1,4,2,512]{4,3,2,1,0:T(2,128)} %get-tuple-element.94), channel_id=1, source_target_pairs={{0,2},{2,4},{4,6},{6,8},{8,10},{10,12},{12,14},{14,16},{16,18},{18... | collective-permute-start | bytes 98312 | tf_op jit(solution)/shard_map/ppermute | solution.py:23
  474.6 30.2 %collective-permute-start.24 = (f32[2,1,4,2,512]{4,3,2,1,0:T(2,128)}, f32[2,1,4,2,512]{4,3,2,1,0:T(2,128)}, u32[]{:S(2)}, u32[]{:S(2)}) collective-permute-start(f32[2,1,4,2,512]{4,3,2,1,0:T(2,128)} %get-tuple-element.95), channel_id=1, source_target_pairs={{2,0},{4,2},{6,4},{8,6},{10,8},{12,10},{14,12},{16,14},{18,16},{20... | collective-permute-start | bytes 98312 | tf_op jit(solution)/shard_map/ppermute | solution.py:25
  504.7 51.8 %all-reduce.17.cloned.1.call-start = ((), (), s32[]{:S(2)}) async-start(), calls=%async_computation.23 | async-start | bytes 262144 | tf_op jit(solution)/shard_map/psum | solution.py:178
  506.1 7.4 collective-permute-start.25
  507.4 6.2 collective-permute-start.26
  512.7 11.0 %collective-permute-start.18 = (f32[64,512]{1,0:T(8,128)}, f32[64,512]{1,0:T(8,128)}, u32[]{:S(2)}, u32[]{:S(2)}) collective-permute-start(f32[64,512]{1,0:T(8,128)} %slice_bitcast_fusion.14), channel_id=1, source_target_pairs={{0,128},{128,0},{1,129},{129,1},{2,130},{130,2},{3,131},{131,3},{4... | collective-permute-start | bytes 393224 | tf_op jit(solution)/shard_map/ppermute | solution.py:33
  521.1 65.3 %reduce-scatter.19.cloned.1.call-start = ((), (), s32[]{:S(2)}) async-start(), calls=%async_computation.24 | async-start | bytes 393216 | tf_op jit(solution)/shard_map/reduce_scatter | solution.py:206
  574.1 5.4 collective-permute-start.28
  581.2 29.3 %collective-permute-start.30 = (f32[1,4,68,2]{3,2,1,0:T(8,128)}, f32[1,4,68,2]{3,2,1,0:T(8,128)}, u32[]{:S(2)}, u32[]{:S(2)}) collective-permute-start(f32[1,4,68,2]{3,2,1,0:T(8,128)} %get-tuple-element.102), channel_id=1, source_target_pairs={{1,0},{3,2},{5,4},{7,6},{9,8},{11,10},{13,12},{15,14},{17,16},{19,... | collective-permute-start | bytes 6536 | tf_op jit(solution)/shard_map/ppermute | solution.py:25
  588.4 29.2 %all-to-all-start.5 = ((f32[64,1,512]{2,1,0:T(1,128)}), f32[64,1,512]{2,1,0:T(1,128)S(1)}, u32[]{:S(2)}, u32[]{:S(2)}) async-start(f32[64,1,512]{2,1,0:T(1,128)} %reshape.599), calls=%async_computation.11 | async-start | bytes 262144 | tf_op jit(solution)/shard_map/all_to_all | solution.py:209
  609.2 45.0 %collective-permute-start.31 = (f32[1,4,68,2]{3,2,1,0:T(8,128)}, f32[1,4,68,2]{3,2,1,0:T(8,128)}, u32[]{:S(2)}, u32[]{:S(2)}) collective-permute-start(f32[1,4,68,2]{3,2,1,0:T(8,128)} %get-tuple-element.103), channel_id=1, source_target_pairs={{0,1},{2,3},{4,5},{6,7},{8,9},{10,11},{12,13},{14,15},{16,17},{18,... | collective-permute-start | bytes 6536 | tf_op jit(solution)/shard_map/ppermute | solution.py:23
  647.2 18.4 %all-to-all-start.6 = ((f32[64,1,512]{2,1,0:T(1,128)}), f32[64,1,512]{2,1,0:T(1,128)S(1)}, u32[]{:S(2)}, u32[]{:S(2)}) async-start(f32[64,1,512]{2,1,0:T(1,128)} %reshape.601), calls=%async_computation.12 | async-start | bytes 262144 | tf_op jit(solution)/shard_map/all_to_all | solution.py:173
  654.1 45.3 %reduce-scatter.21.cloned.1.call-start = ((), (), s32[]{:S(2)}) async-start(), calls=%async_computation.25 | async-start | bytes 393216 | tf_op jit(solution)/shard_map/reduce_scatter | solution.py:177
  690.0 44.9 %all-reduce.19.cloned.1.call-start = ((), (), s32[]{:S(2)}) async-start(), calls=%async_computation.26 | async-start | bytes 262144 | tf_op jit(solution)/shard_map/psum | solution.py:178
  693.2 6.3 collective-permute-start.32
  696.9 12.1 %collective-permute-start.27 = (f32[64,512]{1,0:T(8,128)S(1)}, f32[64,512]{1,0:T(8,128)S(1)}, u32[]{:S(2)}, u32[]{:S(2)}) collective-permute-start(f32[64,512]{1,0:T(8,128)S(1)} %slice_bitcast_fusion.9), channel_id=1, source_target_pairs={{0,128},{128,0},{1,129},{129,1},{2,130},{130,2},{3,131},{131,3},{4... | collective-permute-start | bytes 393224 | tf_op jit(solution)/shard_map/ppermute | solution.py:33
  699.5 63.0 %reduce-scatter.23.cloned.1.call-start = ((), (), s32[]{:S(2)}) async-start(), calls=%async_computation.27 | async-start | bytes 393216 | tf_op jit(solution)/shard_map/reduce_scatter | solution.py:206
  701.2 46.5 %collective-permute-start.34 = (f32[2,1,4,68,2]{4,3,2,1,0:T(8,128)}, f32[2,1,4,68,2]{4,3,2,1,0:T(8,128)S(1)}, u32[]{:S(2)}, u32[]{:S(2)}) collective-permute-start(f32[2,1,4,68,2]{4,3,2,1,0:T(8,128)} %get-tuple-element.84), channel_id=1, source_target_pairs={{0,1},{2,3},{4,5},{6,7},{8,9},{10,11},{12,13},{14,15},{16,17},{18,... | collective-permute-start | bytes 13064 | tf_op jit(solution)/shard_map/ppermute | solution.py:23
  702.5 45.2 %collective-permute-start.35 = (f32[2,1,4,68,2]{4,3,2,1,0:T(8,128)}, f32[2,1,4,68,2]{4,3,2,1,0:T(8,128)S(1)}, u32[]{:S(2)}, u32[]{:S(2)}) collective-permute-start(f32[2,1,4,68,2]{4,3,2,1,0:T(8,128)} %get-tuple-element.85), channel_id=1, source_target_pairs={{1,0},{3,2},{5,4},{7,6},{9,8},{11,10},{13,12},{15,14},{17,16},{19,... | collective-permute-start | bytes 13064 | tf_op jit(solution)/shard_map/ppermute | solution.py:25
  764.5 24.4 %all-to-all-start.7 = ((f32[64,1,512]{2,1,0:T(1,128)}), f32[64,1,512]{2,1,0:T(1,128)S(1)}, u32[]{:S(2)}, u32[]{:S(2)}) async-start(f32[64,1,512]{2,1,0:T(1,128)} %reshape.603), calls=%async_computation.15 | async-start | bytes 262144 | tf_op jit(solution)/shard_map/all_to_all | solution.py:209
  (58 other events, 1054.9 us)
Sparse Core Ops, SparseCore 0:
  93.5 17.6 reduce-scatter.8
  115.3 35.8 all-reduce.12
  164.1 14.6 reduce-scatter.10
  308.6 16.7 reduce-scatter.12
  327.8 32.8 all-reduce.14
  380.1 18.4 reduce-scatter.14
  504.8 16.1 reduce-scatter.16
  523.6 32.8 all-reduce.16
  569.5 14.6 reduce-scatter.18
  690.1 9.2 reduce-scatter.20
  702.0 32.8 all-reduce.18
  747.8 14.6 reduce-scatter.22
where the time goes:
time: 815 us; the launch traced here: 804 us
  waiting for transfers between devices  205 us (25%)
  starting transfers between devices  197 us (24%)
  local copies, waits for them, and re-layouts  159 us (20%)
  matrix products  123 us (15%)
  other arithmetic  104 us (13%)
  between operations  16.4 us (2%)
    psum x4, waiting for transfers between devices, per_device(): relief = lax.psum(own_depth, 'grp') * scale_back  125 us
    unnamed x116, local copies, waits for them, and re-layouts  73.8 us
    all_to_all x4, starting transfers between devices, per_device(): lax.all_to_all(by_modes, 'gx', split_axis=0, concat_axis=2, tiled=True)  59.3 us
    ppermute x16, starting transfers between devices, extended(): lax.ppermute(head, axis, [((i + 1) % count, i) for i in range(ends)])  50.3 us
    ppermute x16, starting transfers between devices, extended(): lax.ppermute(tail, axis, [(i, (i + 1) % count) for i in range(ends)])  38.2 us
    all_to_all x4, starting transfers between devices, per_device(): lax.all_to_all(in_space, 'gx', split_axis=2, concat_axis=0, tiled=True)  35.7 us
    all_to_all x4, waiting for transfers between devices, per_device(): lax.all_to_all(by_modes, 'gx', split_axis=0, concat_axis=2, tiled=True)  27.6 us
    all_to_all x9, local copies, waits for them, and re-layouts, per_device(): lax.all_to_all(in_space, 'gx', split_axis=2, concat_axis=0, tiled=True)  22.7 us
  transfers between devices with their start and end apart: 56, of which 22 were waited for; matrix products, arithmetic and copies ran while one was open for 28% of the time, Pallas kernels for 0%

commit v1 on v0

--- a/solution.py
+++ b/solution.py
@@ -170,7 +170,11 @@
     for step_number in range(NSTEP):
         summed = jnp.sum(weights[:, :, None, :] * lagged, axis=0)
         in_space = strike_inverse(summed, strike_devices, strike_rows)
-        by_rows = lax.all_to_all(in_space, "gx", split_axis=2, concat_axis=0, tiled=True)
+        mat_out = lax.axis_size("gx")
+        arr_out = jnp.split(in_space, mat_out, axis=2)
+        n_now = jnp.stack(arr_out)
+        local_part = lax.all_to_all(n_now, "gx", split_axis=0, concat_axis=0)
+        by_rows = jnp.concatenate(local_part, 0)
         partial_value = jnp.einsum(
             "jy,jz->yz", by_rows[:, 0], back_cos, precision=FULL_PRECISION
         ) - jnp.einsum("jy,jz->yz", by_rows[:, 1], back_sin, precision=FULL_PRECISION)

time: 815 us -> 724 us (0.89)
  local copies, waits for them, and re-layouts: 159 us -> 75.1 us
  starting transfers between devices: 197 us -> 187 us
    unnamed x116 -> x374, local copies, waits for them, and re-layouts: 73.8 us -> 28.2 us
    all_to_all x9 -> x5, local copies, waits for them, and re-layouts: 22.7 us -> 0.77 us  [per_device(): local_part = lax.all_to_all(n_now, 'gx', split_axis=0, concat_axis=0)]
    another operation x12, local copies, waits for them, and re-layouts: 22.5 us -> 10.7 us  [strike_inverse(): jnp.stack([real_part.reshape(planes_count, total_count), imag_part.reshap...]
    ppermute x4, starting transfers between devices: 12.7 us -> 2.77 us  [from_partner(): lax.ppermute(x, axis, [(i, i ^ 1 << stride) for i in range(lax.axis_size(...]
  transfers between devices with their start and end apart: 56 -> 56, of which waited for: 22 -> 23; matrix products, arithmetic and copies ran while one was open for 28% -> 24% of each run, Pallas kernels for 0% -> 0%
where the time goes in v1:
time: 724 us; the launch traced here: 715 us
  waiting for transfers between devices  210 us (29%)
  starting transfers between devices  187 us (26%)
  matrix products  127 us (18%)
  other arithmetic  98.6 us (14%)
  local copies, waits for them, and re-layouts  75.1 us (10%)
  between operations  16.6 us (2%)
    psum x4, waiting for transfers between devices, per_device(): relief = lax.psum(own_depth, 'grp') * scale_back  123 us
    all_to_all x4, starting transfers between devices, per_device(): lax.all_to_all(by_modes, 'gx', split_axis=0, concat_axis=2, tiled=True)  59.1 us
    ppermute x16, starting transfers between devices, extended(): lax.ppermute(head, axis, [((i + 1) % count, i) for i in range(ends)])  51 us
    ppermute x16, starting transfers between devices, extended(): lax.ppermute(tail, axis, [(i, (i + 1) % count) for i in range(ends)])  38.3 us
    all_to_all x4, starting transfers between devices, per_device(): local_part = lax.all_to_all(n_now, 'gx', split_axis=0, concat_axis=0)  35.1 us
    unnamed x374, local copies, waits for them, and re-layouts  28.2 us
    all_to_all x4, waiting for transfers between devices, per_device(): lax.all_to_all(by_modes, 'gx', split_axis=0, concat_axis=2, tiled=True)  27.6 us
    dot_general x4, matrix products, per_device(): jnp.einsum('jy,jz->yz', by_rows[:, 1], back_sin, precision=FULL_PRECISION)  21.5 us
  transfers between devices with their start and end apart: 56, of which 23 were waited for; matrix products, arithmetic and copies ran while one was open for 24% of the time, Pallas kernels for 0%

profile of v1, /device:TPU:1, one launch (start us, length us, event | category | flops | bytes accessed | tf_op | source)
XLA Modules:
  0.0 714.8 jit_solution(5860039635598680984)
XLA Ops:
  9.7 4.6 collective-permute-start.2
  25.8 18.5 %all-to-all-start = ((f32[64,1,512]{2,1,0:T(1,128)}), f32[64,1,512]{2,1,0:T(1,128)S(1)}, u32[]{:S(2)}, u32[]{:S(2)}) async-start(f32[64,1,512]{2,1,0:T(1,128)} %reshape.605), calls=%async_computation | async-start | bytes 262144 | tf_op jit(solution)/shard_map/all_to_all | solution.py:176
  62.7 4.6 fusion.195
  67.3 5.4 convolution_subtract_fusion.3
  85.1 5.3 reduce-scatter.9.cloned.1.call-done
  93.5 32.4 %all-reduce.13.cloned.1.call-done = f32[64,512]{1,0:T(8,128)} async-done(((f32[64,512]{1,0:T(8,128)}), f32[64,512]{1,0:T(8,128)}) %all-reduce.13.cloned.1.call-update) | async-done | bytes 131088 | tf_op jit(solution)/shard_map/psum | solution.py:182
  128.1 5.0 convolution_bitcast_fusion.6
  133.1 4.9 convolution_bitcast_fusion.7
  138.7 5.1 fusion.70
  150.8 5.0 collective-permute-start.12
  162.7 17.2 %all-to-all-start.1 = ((f32[64,1,512]{2,1,0:T(1,128)}), f32[64,1,512]{2,1,0:T(1,128)S(1)}, u32[]{:S(2)}, u32[]{:S(2)}) async-start(f32[64,1,512]{2,1,0:T(1,128)} %reshape.607), calls=%async_computation.3 | async-start | bytes 262144 | tf_op jit(solution)/shard_map/all_to_all | solution.py:213
  183.3 8.0 %all-to-all-done.1 = f32[64,1,512]{2,1,0:T(1,128)S(1)} async-done(((f32[64,1,512]{2,1,0:T(1,128)}), f32[64,1,512]{2,1,0:T(1,128)S(1)}, u32[]{:S(2)}, u32[]{:S(2)}) %all-to-all-start.1) | async-done | bytes 131104 | tf_op jit(solution)/shard_map/all_to_all | solution.py:213
  235.2 5.0 all-to-all-start.2
  247.4 4.2 all-to-all-done.2
  252.8 4.6 fusion.193
  257.4 5.4 convolution_subtract_fusion.2
  265.5 6.3 collective-permute-start.17
  275.1 4.6 reduce-scatter.13.cloned.1.call-done
  282.4 32.7 %all-reduce.15.cloned.1.call-done = f32[64,512]{1,0:T(8,128)} async-done(((f32[64,512]{1,0:T(8,128)}), f32[64,512]{1,0:T(8,128)}) %all-reduce.15.cloned.1.call-update) | async-done | bytes 131088 | tf_op jit(solution)/shard_map/psum | solution.py:182
  317.2 5.0 convolution_bitcast_fusion.4
  322.3 4.9 convolution_bitcast_fusion.5
  335.2 4.6 collective-permute-start.21
  345.7 7.2 %reduce-scatter.15.cloned.1.call-done = f32[256,2,64]{0,2,1:T(8,128)} async-done(((f32[512,2,64]{0,2,1:T(8,128)}), f32[256,2,64]{0,2,1:T(8,128)}) %reduce-scatter.15.cloned.1.call-update) | async-done | bytes 131088 | tf_op jit(solution)/shard_map/reduce_scatter | solution.py:210
  354.9 12.3 %all-to-all-start.3 = ((f32[64,1,512]{2,1,0:T(1,128)}), f32[64,1,512]{2,1,0:T(1,128)S(1)}, u32[]{:S(2)}, u32[]{:S(2)}) async-start(f32[64,1,512]{2,1,0:T(1,128)} %reshape.611), calls=%async_computation.7 | async-start | bytes 262144 | tf_op jit(solution)/shard_map/all_to_all | solution.py:213
  370.6 8.7 %all-to-all-done.3 = f32[64,1,512]{2,1,0:T(1,128)S(1)} async-done(((f32[64,1,512]{2,1,0:T(1,128)}), f32[64,1,512]{2,1,0:T(1,128)S(1)}, u32[]{:S(2)}, u32[]{:S(2)}) %all-to-all-start.3) | async-done | bytes 131104 | tf_op jit(solution)/shard_map/all_to_all | solution.py:213
  402.5 4.7 all-to-all-start.4
  419.8 4.6 fusion.191
  424.5 5.4 convolution_subtract_fusion.1
  432.6 4.8 collective-permute-start.26
  440.4 5.4 reduce-scatter.17.cloned.1.call-done
  448.7 32.6 %all-reduce.17.cloned.1.call-done = f32[64,512]{1,0:T(8,128)} async-done(((f32[64,512]{1,0:T(8,128)}), f32[64,512]{1,0:T(8,128)}) %all-reduce.17.cloned.1.call-update) | async-done | bytes 131088 | tf_op jit(solution)/shard_map/psum | solution.py:182
  483.6 5.0 convolution_bitcast_fusion.2
  488.5 4.9 convolution_bitcast_fusion.3
  494.2 4.5 fusion.102
  505.7 5.3 collective-permute-start.30
  513.0 17.2 %all-to-all-start.5 = ((f32[64,1,512]{2,1,0:T(1,128)}), f32[64,1,512]{2,1,0:T(1,128)S(1)}, u32[]{:S(2)}, u32[]{:S(2)}) async-start(f32[64,1,512]{2,1,0:T(1,128)} %reshape.615), calls=%async_computation.11 | async-start | bytes 262144 | tf_op jit(solution)/shard_map/all_to_all | solution.py:213
  537.0 5.3 all-to-all-done.5
  571.5 6.9 all-to-all-start.6
  581.1 8.7 %all-to-all-done.6 = f32[64,1,512]{2,1,0:T(1,128)S(1)} async-done(((f32[64,1,512]{2,1,0:T(1,128)}), f32[64,1,512]{2,1,0:T(1,128)S(1)}, u32[]{:S(2)}, u32[]{:S(2)}) %all-to-all-start.6) | async-done | bytes 131104 | tf_op jit(solution)/shard_map/all_to_all | solution.py:176
  591.1 4.6 fusion.189
  595.7 5.4 convolution_subtract_fusion
  613.4 6.8 collective-permute-start.35
  620.2 25.8 %all-reduce.19.cloned.1.call-done = f32[64,512]{1,0:T(8,128)} async-done(((f32[64,512]{1,0:T(8,128)}), f32[64,512]{1,0:T(8,128)}) %all-reduce.19.cloned.1.call-update) | async-done | bytes 131088 | tf_op jit(solution)/shard_map/psum | solution.py:182
  648.2 5.0 convolution_bitcast_fusion
  653.2 4.9 convolution_bitcast_fusion.1
  661.2 12.4 %reduce-scatter.23.cloned.1.call-done = f32[256,2,64]{0,2,1:T(8,128)} async-done(((f32[512,2,64]{0,2,1:T(8,128)}), f32[256,2,64]{0,2,1:T(8,128)}) %reduce-scatter.23.cloned.1.call-update) | async-done | bytes 131088 | tf_op jit(solution)/shard_map/reduce_scatter | solution.py:210
  675.6 12.3 %all-to-all-start.7 = ((f32[64,1,512]{2,1,0:T(1,128)}), f32[64,1,512]{2,1,0:T(1,128)S(1)}, u32[]{:S(2)}, u32[]{:S(2)}) async-start(f32[64,1,512]{2,1,0:T(1,128)} %reshape.619), calls=%async_computation.15 | async-start | bytes 262144 | tf_op jit(solution)/shard_map/all_to_all | solution.py:213
  694.4 5.6 all-to-all-done.7
  (683 shorter events, 278.5 us)
Async XLA Ops:
  8.4 35.9 %collective-permute-start.1 = (f32[1,4,2,512]{3,2,1,0:T(2,128)S(1)}, f32[1,4,2,512]{3,2,1,0:T(2,128)S(1)}, u32[]{:S(2)}, u32[]{:S(2)}) collective-permute-start(f32[1,4,2,512]{3,2,1,0:T(2,128)S(1)} %get-tuple-element.127), channel_id=1, source_target_pairs={{2,0},{4,2},{6,4},{8,6},{10,8},{12,10},{14,12},{16,14},{18,16},{20... | collective-permute-start | bytes 49160 | tf_op jit(solution)/shard_map/ppermute | solution.py:25
  9.7 34.6 %collective-permute-start.2 = (f32[1,4,2,512]{3,2,1,0:T(2,128)S(1)}, f32[1,4,2,512]{3,2,1,0:T(2,128)S(1)}, u32[]{:S(2)}, u32[]{:S(2)}) collective-permute-start(f32[1,4,2,512]{3,2,1,0:T(2,128)S(1)} %get-tuple-element.126), channel_id=1, source_target_pairs={{0,2},{2,4},{4,6},{6,8},{8,10},{10,12},{12,14},{14,16},{16,18},{18... | collective-permute-start | bytes 49160 | tf_op jit(solution)/shard_map/ppermute | solution.py:23
  25.8 33.6 %all-to-all-start = ((f32[64,1,512]{2,1,0:T(1,128)}), f32[64,1,512]{2,1,0:T(1,128)S(1)}, u32[]{:S(2)}, u32[]{:S(2)}) async-start(f32[64,1,512]{2,1,0:T(1,128)} %reshape.605), calls=%async_computation | async-start | bytes 262144 | tf_op jit(solution)/shard_map/all_to_all | solution.py:176
  44.3 46.2 %reduce-scatter.9.cloned.1.call-start = ((), (), s32[]{:S(2)}) async-start(), calls=%async_computation.16 | async-start | bytes 393216 | tf_op jit(solution)/shard_map/reduce_scatter | solution.py:181
  54.6 19.5 %collective-permute-start.5 = (f32[2,1,4,2,512]{4,3,2,1,0:T(2,128)}, f32[2,1,4,2,512]{4,3,2,1,0:T(2,128)S(1)}, u32[]{:S(2)}, u32[]{:S(2)}) collective-permute-start(f32[2,1,4,2,512]{4,3,2,1,0:T(2,128)} %get-tuple-element.98), channel_id=1, source_target_pairs={{0,2},{2,4},{4,6},{6,8},{8,10},{10,12},{12,14},{14,16},{16,18},{18... | collective-permute-start | bytes 98312 | tf_op jit(solution)/shard_map/ppermute | solution.py:23
  57.8 16.3 %collective-permute-start.6 = (f32[2,1,4,2,512]{4,3,2,1,0:T(2,128)}, f32[2,1,4,2,512]{4,3,2,1,0:T(2,128)S(1)}, u32[]{:S(2)}, u32[]{:S(2)}) collective-permute-start(f32[2,1,4,2,512]{4,3,2,1,0:T(2,128)} %get-tuple-element.99), channel_id=1, source_target_pairs={{2,0},{4,2},{6,4},{8,6},{10,8},{12,10},{14,12},{16,14},{18,16},{20... | collective-permute-start | bytes 98312 | tf_op jit(solution)/shard_map/ppermute | solution.py:25
  72.7 53.2 %all-reduce.13.cloned.1.call-start = ((), (), s32[]{:S(2)}) async-start(), calls=%async_computation.17 | async-start | bytes 262144 | tf_op jit(solution)/shard_map/psum | solution.py:182
  73.4 20.1 %collective-permute-start = (f32[64,512]{1,0:T(8,128)}, f32[64,512]{1,0:T(8,128)}, u32[]{:S(2)}, u32[]{:S(2)}) collective-permute-start(f32[64,512]{1,0:T(8,128)} %slice_bitcast_fusion.24), channel_id=1, source_target_pairs={{0,128},{128,0},{1,129},{129,1},{2,130},{130,2},{3,131},{131,3},{4... | collective-permute-start | bytes 393224 | tf_op jit(solution)/shard_map/ppermute | solution.py:33
  90.5 70.3 %reduce-scatter.11.cloned.1.call-start = ((), (), s32[]{:S(2)}) async-start(), calls=%async_computation.18 | async-start | bytes 393216 | tf_op jit(solution)/shard_map/reduce_scatter | solution.py:210
  143.9 5.3 collective-permute-start.10
  150.8 8.0 %collective-permute-start.12 = (f32[1,4,68,2]{3,2,1,0:T(8,128)S(1)}, f32[1,4,68,2]{3,2,1,0:T(8,128)}, u32[]{:S(2)}, u32[]{:S(2)}) collective-permute-start(f32[1,4,68,2]{3,2,1,0:T(8,128)S(1)} %get-tuple-element.110), channel_id=1, source_target_pairs={{1,0},{3,2},{5,4},{7,6},{9,8},{11,10},{13,12},{15,14},{17,16},{19,... | collective-permute-start | bytes 6536 | tf_op jit(solution)/shard_map/ppermute | solution.py:25
  157.5 22.4 %collective-permute-start.13 = (f32[1,4,68,2]{3,2,1,0:T(8,128)}, f32[1,4,68,2]{3,2,1,0:T(8,128)}, u32[]{:S(2)}, u32[]{:S(2)}) collective-permute-start(f32[1,4,68,2]{3,2,1,0:T(8,128)} %get-tuple-element.111), channel_id=1, source_target_pairs={{0,1},{2,3},{4,5},{6,7},{8,9},{10,11},{12,13},{14,15},{16,17},{18,... | collective-permute-start | bytes 6536 | tf_op jit(solution)/shard_map/ppermute | solution.py:23
  162.7 28.6 %all-to-all-start.1 = ((f32[64,1,512]{2,1,0:T(1,128)}), f32[64,1,512]{2,1,0:T(1,128)S(1)}, u32[]{:S(2)}, u32[]{:S(2)}) async-start(f32[64,1,512]{2,1,0:T(1,128)} %reshape.607), calls=%async_computation.3 | async-start | bytes 262144 | tf_op jit(solution)/shard_map/all_to_all | solution.py:213
  235.2 16.4 %all-to-all-start.2 = ((f32[64,1,512]{2,1,0:T(1,128)}), f32[64,1,512]{2,1,0:T(1,128)S(1)}, u32[]{:S(2)}, u32[]{:S(2)}) async-start(f32[64,1,512]{2,1,0:T(1,128)} %reshape.609), calls=%async_computation.4 | async-start | bytes 262144 | tf_op jit(solution)/shard_map/all_to_all | solution.py:176
  240.2 39.6 %reduce-scatter.13.cloned.1.call-start = ((), (), s32[]{:S(2)}) async-start(), calls=%async_computation.19 | async-start | bytes 393216 | tf_op jit(solution)/shard_map/reduce_scatter | solution.py:181
  243.3 19.6 %collective-permute-start.14 = (f32[2,1,4,2,512]{4,3,2,1,0:T(2,128)S(1)}, f32[2,1,4,2,512]{4,3,2,1,0:T(2,128)S(1)}, u32[]{:S(2)}, u32[]{:S(2)}) collective-permute-start(f32[2,1,4,2,512]{4,3,2,1,0:T(2,128)S(1)} %get-tuple-element.96), channel_id=1, source_target_pairs={{0,2},{2,4},{4,6},{6,8},{8,10},{10,12},{12,14},{14,16},{16,18},{18... | collective-permute-start | bytes 98312 | tf_op jit(solution)/shard_map/ppermute | solution.py:23
  246.1 16.8 %collective-permute-start.15 = (f32[2,1,4,2,512]{4,3,2,1,0:T(2,128)S(1)}, f32[2,1,4,2,512]{4,3,2,1,0:T(2,128)S(1)}, u32[]{:S(2)}, u32[]{:S(2)}) collective-permute-start(f32[2,1,4,2,512]{4,3,2,1,0:T(2,128)S(1)} %get-tuple-element.97), channel_id=1, source_target_pairs={{2,0},{4,2},{6,4},{8,6},{10,8},{12,10},{14,12},{16,14},{18,16},{20... | collective-permute-start | bytes 98312 | tf_op jit(solution)/shard_map/ppermute | solution.py:25
  262.8 52.2 %all-reduce.15.cloned.1.call-start = ((), (), s32[]{:S(2)}) async-start(), calls=%async_computation.20 | async-start | bytes 262144 | tf_op jit(solution)/shard_map/psum | solution.py:182
  264.2 9.1 %collective-permute-start.16 = (f32[2,1,4,68,2]{4,3,2,1,0:T(8,128)S(1)}, f32[2,1,4,68,2]{4,3,2,1,0:T(8,128)S(1)}, u32[]{:S(2)}, u32[]{:S(2)}) collective-permute-start(f32[2,1,4,68,2]{4,3,2,1,0:T(8,128)S(1)} %get-tuple-element.88), channel_id=1, source_target_pairs={{0,1},{2,3},{4,5},{6,7},{8,9},{10,11},{12,13},{14,15},{16,17},{18,... | collective-permute-start | bytes 13064 | tf_op jit(solution)/shard_map/ppermute | solution.py:23
  265.5 7.8 %collective-permute-start.17 = (f32[2,1,4,68,2]{4,3,2,1,0:T(8,128)S(1)}, f32[2,1,4,68,2]{4,3,2,1,0:T(8,128)S(1)}, u32[]{:S(2)}, u32[]{:S(2)}) collective-permute-start(f32[2,1,4,68,2]{4,3,2,1,0:T(8,128)S(1)} %get-tuple-element.89), channel_id=1, source_target_pairs={{1,0},{3,2},{5,4},{7,6},{9,8},{11,10},{13,12},{15,14},{17,16},{19,... | collective-permute-start | bytes 13064 | tf_op jit(solution)/shard_map/ppermute | solution.py:25
  272.5 9.9 %collective-permute-start.9 = (f32[64,512]{1,0:T(8,128)}, f32[64,512]{1,0:T(8,128)S(1)}, u32[]{:S(2)}, u32[]{:S(2)}) collective-permute-start(f32[64,512]{1,0:T(8,128)} %slice_bitcast_fusion.19), channel_id=1, source_target_pairs={{0,128},{128,0},{1,129},{129,1},{2,130},{130,2},{3,131},{131,3},{4... | collective-permute-start | bytes 393224 | tf_op jit(solution)/shard_map/ppermute | solution.py:33
  279.8 73.1 %reduce-scatter.15.cloned.1.call-start = ((), (), s32[]{:S(2)}) async-start(), calls=%async_computation.21 | async-start | bytes 393216 | tf_op jit(solution)/shard_map/reduce_scatter | solution.py:210
  328.3 6.1 collective-permute-start.19
  335.2 9.6 %collective-permute-start.21 = (f32[1,4,68,2]{3,2,1,0:T(8,128)S(1)}, f32[1,4,68,2]{3,2,1,0:T(8,128)S(1)}, u32[]{:S(2)}, u32[]{:S(2)}) collective-permute-start(f32[1,4,68,2]{3,2,1,0:T(8,128)S(1)} %get-tuple-element.106), channel_id=1, source_target_pairs={{1,0},{3,2},{5,4},{7,6},{9,8},{11,10},{13,12},{15,14},{17,16},{19,... | collective-permute-start | bytes 6536 | tf_op jit(solution)/shard_map/ppermute | solution.py:25
  343.4 23.9 %collective-permute-start.22 = (f32[1,4,68,2]{3,2,1,0:T(8,128)}, f32[1,4,68,2]{3,2,1,0:T(8,128)}, u32[]{:S(2)}, u32[]{:S(2)}) collective-permute-start(f32[1,4,68,2]{3,2,1,0:T(8,128)} %get-tuple-element.107), channel_id=1, source_target_pairs={{0,1},{2,3},{4,5},{6,7},{8,9},{10,11},{12,13},{14,15},{16,17},{18,... | collective-permute-start | bytes 6536 | tf_op jit(solution)/shard_map/ppermute | solution.py:23
  354.9 24.4 %all-to-all-start.3 = ((f32[64,1,512]{2,1,0:T(1,128)}), f32[64,1,512]{2,1,0:T(1,128)S(1)}, u32[]{:S(2)}, u32[]{:S(2)}) async-start(f32[64,1,512]{2,1,0:T(1,128)} %reshape.611), calls=%async_computation.7 | async-start | bytes 262144 | tf_op jit(solution)/shard_map/all_to_all | solution.py:213
  402.5 16.1 %all-to-all-start.4 = ((f32[64,1,512]{2,1,0:T(1,128)}), f32[64,1,512]{2,1,0:T(1,128)S(1)}, u32[]{:S(2)}, u32[]{:S(2)}) async-start(f32[64,1,512]{2,1,0:T(1,128)} %reshape.613), calls=%async_computation.8 | async-start | bytes 262144 | tf_op jit(solution)/shard_map/all_to_all | solution.py:176
  407.2 38.7 %reduce-scatter.17.cloned.1.call-start = ((), (), s32[]{:S(2)}) async-start(), calls=%async_computation.22 | async-start | bytes 393216 | tf_op jit(solution)/shard_map/reduce_scatter | solution.py:181
  410.7 19.3 %collective-permute-start.23 = (f32[2,1,4,2,512]{4,3,2,1,0:T(2,128)S(1)}, f32[2,1,4,2,512]{4,3,2,1,0:T(2,128)S(1)}, u32[]{:S(2)}, u32[]{:S(2)}) collective-permute-start(f32[2,1,4,2,512]{4,3,2,1,0:T(2,128)S(1)} %get-tuple-element.94), channel_id=1, source_target_pairs={{0,2},{2,4},{4,6},{6,8},{8,10},{10,12},{12,14},{14,16},{16,18},{18... | collective-permute-start | bytes 98312 | tf_op jit(solution)/shard_map/ppermute | solution.py:23
  413.6 16.3 %collective-permute-start.24 = (f32[2,1,4,2,512]{4,3,2,1,0:T(2,128)S(1)}, f32[2,1,4,2,512]{4,3,2,1,0:T(2,128)S(1)}, u32[]{:S(2)}, u32[]{:S(2)}) collective-permute-start(f32[2,1,4,2,512]{4,3,2,1,0:T(2,128)S(1)} %get-tuple-element.95), channel_id=1, source_target_pairs={{2,0},{4,2},{6,4},{8,6},{10,8},{12,10},{14,12},{16,14},{18,16},{20... | collective-permute-start | bytes 98312 | tf_op jit(solution)/shard_map/ppermute | solution.py:25
  429.9 51.4 %all-reduce.17.cloned.1.call-start = ((), (), s32[]{:S(2)}) async-start(), calls=%async_computation.23 | async-start | bytes 262144 | tf_op jit(solution)/shard_map/psum | solution.py:182
  431.3 7.4 %collective-permute-start.25 = (f32[2,1,4,68,2]{4,3,2,1,0:T(8,128)S(1)}, f32[2,1,4,68,2]{4,3,2,1,0:T(8,128)S(1)}, u32[]{:S(2)}, u32[]{:S(2)}) collective-permute-start(f32[2,1,4,68,2]{4,3,2,1,0:T(8,128)S(1)} %get-tuple-element.86), channel_id=1, source_target_pairs={{0,1},{2,3},{4,5},{6,7},{8,9},{10,11},{12,13},{14,15},{16,17},{18,... | collective-permute-start | bytes 13064 | tf_op jit(solution)/shard_map/ppermute | solution.py:23
  432.6 6.1 collective-permute-start.26
  438.0 10.7 %collective-permute-start.18 = (f32[64,512]{1,0:T(8,128)}, f32[64,512]{1,0:T(8,128)}, u32[]{:S(2)}, u32[]{:S(2)}) collective-permute-start(f32[64,512]{1,0:T(8,128)} %slice_bitcast_fusion.14), channel_id=1, source_target_pairs={{0,128},{128,0},{1,129},{129,1},{2,130},{130,2},{3,131},{131,3},{4... | collective-permute-start | bytes 393224 | tf_op jit(solution)/shard_map/ppermute | solution.py:33
  445.9 65.2 %reduce-scatter.19.cloned.1.call-start = ((), (), s32[]{:S(2)}) async-start(), calls=%async_computation.24 | async-start | bytes 393216 | tf_op jit(solution)/shard_map/reduce_scatter | solution.py:210
  498.7 5.4 collective-permute-start.28
  505.7 29.3 %collective-permute-start.30 = (f32[1,4,68,2]{3,2,1,0:T(8,128)}, f32[1,4,68,2]{3,2,1,0:T(8,128)}, u32[]{:S(2)}, u32[]{:S(2)}) collective-permute-start(f32[1,4,68,2]{3,2,1,0:T(8,128)} %get-tuple-element.102), channel_id=1, source_target_pairs={{1,0},{3,2},{5,4},{7,6},{9,8},{11,10},{13,12},{15,14},{17,16},{19,... | collective-permute-start | bytes 6536 | tf_op jit(solution)/shard_map/ppermute | solution.py:25
  513.0 29.2 %all-to-all-start.5 = ((f32[64,1,512]{2,1,0:T(1,128)}), f32[64,1,512]{2,1,0:T(1,128)S(1)}, u32[]{:S(2)}, u32[]{:S(2)}) async-start(f32[64,1,512]{2,1,0:T(1,128)} %reshape.615), calls=%async_computation.11 | async-start | bytes 262144 | tf_op jit(solution)/shard_map/all_to_all | solution.py:213
  533.8 44.7 %collective-permute-start.31 = (f32[1,4,68,2]{3,2,1,0:T(8,128)}, f32[1,4,68,2]{3,2,1,0:T(8,128)}, u32[]{:S(2)}, u32[]{:S(2)}) collective-permute-start(f32[1,4,68,2]{3,2,1,0:T(8,128)} %get-tuple-element.103), channel_id=1, source_target_pairs={{0,1},{2,3},{4,5},{6,7},{8,9},{10,11},{12,13},{14,15},{16,17},{18,... | collective-permute-start | bytes 6536 | tf_op jit(solution)/shard_map/ppermute | solution.py:23
  571.5 18.4 %all-to-all-start.6 = ((f32[64,1,512]{2,1,0:T(1,128)}), f32[64,1,512]{2,1,0:T(1,128)S(1)}, u32[]{:S(2)}, u32[]{:S(2)}) async-start(f32[64,1,512]{2,1,0:T(1,128)} %reshape.617), calls=%async_computation.12 | async-start | bytes 262144 | tf_op jit(solution)/shard_map/all_to_all | solution.py:176
  578.4 32.2 %reduce-scatter.21.cloned.1.call-start = ((), (), s32[]{:S(2)}) async-start(), calls=%async_computation.25 | async-start | bytes 393216 | tf_op jit(solution)/shard_map/reduce_scatter | solution.py:181
  601.1 44.9 %all-reduce.19.cloned.1.call-start = ((), (), s32[]{:S(2)}) async-start(), calls=%async_computation.26 | async-start | bytes 262144 | tf_op jit(solution)/shard_map/psum | solution.py:182
  604.1 6.5 collective-permute-start.32
  607.9 12.3 %collective-permute-start.27 = (f32[64,512]{1,0:T(8,128)S(1)}, f32[64,512]{1,0:T(8,128)S(1)}, u32[]{:S(2)}, u32[]{:S(2)}) collective-permute-start(f32[64,512]{1,0:T(8,128)S(1)} %slice_bitcast_fusion.9), channel_id=1, source_target_pairs={{0,128},{128,0},{1,129},{129,1},{2,130},{130,2},{3,131},{131,3},{4... | collective-permute-start | bytes 393224 | tf_op jit(solution)/shard_map/ppermute | solution.py:33
  610.6 63.1 %reduce-scatter.23.cloned.1.call-start = ((), (), s32[]{:S(2)}) async-start(), calls=%async_computation.27 | async-start | bytes 393216 | tf_op jit(solution)/shard_map/reduce_scatter | solution.py:210
  612.1 46.7 %collective-permute-start.34 = (f32[2,1,4,68,2]{4,3,2,1,0:T(8,128)}, f32[2,1,4,68,2]{4,3,2,1,0:T(8,128)S(1)}, u32[]{:S(2)}, u32[]{:S(2)}) collective-permute-start(f32[2,1,4,68,2]{4,3,2,1,0:T(8,128)} %get-tuple-element.84), channel_id=1, source_target_pairs={{0,1},{2,3},{4,5},{6,7},{8,9},{10,11},{12,13},{14,15},{16,17},{18,... | collective-permute-start | bytes 13064 | tf_op jit(solution)/shard_map/ppermute | solution.py:23
  613.4 45.4 %collective-permute-start.35 = (f32[2,1,4,68,2]{4,3,2,1,0:T(8,128)}, f32[2,1,4,68,2]{4,3,2,1,0:T(8,128)S(1)}, u32[]{:S(2)}, u32[]{:S(2)}) collective-permute-start(f32[2,1,4,68,2]{4,3,2,1,0:T(8,128)} %get-tuple-element.85), channel_id=1, source_target_pairs={{1,0},{3,2},{5,4},{7,6},{9,8},{11,10},{13,12},{15,14},{17,16},{19,... | collective-permute-start | bytes 13064 | tf_op jit(solution)/shard_map/ppermute | solution.py:25
  675.6 24.4 %all-to-all-start.7 = ((f32[64,1,512]{2,1,0:T(1,128)}), f32[64,1,512]{2,1,0:T(1,128)S(1)}, u32[]{:S(2)}, u32[]{:S(2)}) async-start(f32[64,1,512]{2,1,0:T(1,128)} %reshape.619), calls=%async_computation.15 | async-start | bytes 262144 | tf_op jit(solution)/shard_map/all_to_all | solution.py:213
  (59 other events, 1101.9 us)
Sparse Core Ops, SparseCore 0:
  72.8 17.5 reduce-scatter.8
  93.0 32.8 all-reduce.12
  138.8 14.6 reduce-scatter.10
  263.0 16.7 reduce-scatter.12
  282.2 32.8 all-reduce.14
  334.5 18.4 reduce-scatter.14
  430.0 15.8 reduce-scatter.16
  448.4 32.8 all-reduce.16
  494.3 14.6 reduce-scatter.18
  601.2 9.2 reduce-scatter.20
  613.1 32.8 all-reduce.18
  658.9 14.6 reduce-scatter.22
